TPU v7x, 512 devices: a whole 4x4x16 slice. The times are simulated.
512 devices in a mesh: row: 8 (over x, y_lo), col: 4 (over y_hi, core), seq: 16 (over z).
Axes of the slice: x: 4, y: 4 (y_hi: 2, y_lo: 2; y = y_hi * 2 + y_lo), z: 16, core: 2. Of those that a mesh axis runs over, the one named last changes fastest.
Arguments:
- hidden_in: bfloat16 [8, 3072, 6144], P('row', 'seq', 'col'), may hold values from -6 to 6
- projection: bfloat16 [6144, 9216], P(('col', 'seq'), 'row'), may hold values from -0.078125 to 0.078125
Outputs:
- attention: bfloat16 [8, 3072, 3072], P('col', 'seq', 'row')
All inputs are finite; a program needn't handle non-finite values.
Results may differ from a plain program's by a relative error of at most 0.012.
Values may be sent and summed in bfloat16 or wider, within the bound.
A program may use at most 64 MiB of HBM per device.

v0:
```python
import math

import jax
import jax.numpy as jnp
from jax import lax
from jax.sharding import PartitionSpec as P

HD = 128


def entering(x, axis, combine, identity):
    devices, here = (lax.axis_size(axis), lax.axis_index(axis))
    everything = jax.tree.map(
        lambda part, kind: lax.all_gather(part.astype(kind), axis), x, (jnp.bfloat16, jnp.bfloat16)
    )
    start = jax.tree.map(
        lambda part, zero: jnp.broadcast_to(jnp.asarray(zero, part.dtype), part.shape), x, identity
    )

    def turn(k, before):
        reached = k < here
        new = combine(
            before, jax.tree.map(lambda part, own: part[k].astype(own.dtype), everything, x)
        )
        return jax.tree.map(lambda a, b: jnp.where(reached, a, b), new, before)

    return lax.fori_loop(0, devices, turn, start)


def feature_map(rows, angle, factor):
    active = jnp.maximum(rows.astype(jnp.float32), 0.0)
    cosine = jnp.cos(angle)[None, :, None, None]
    sine = jnp.sin(angle)[None, :, None, None]
    joined = jnp.concatenate([active * cosine, active * sine], axis=-1) * factor
    return joined.astype(jnp.bfloat16)


def add_pair(earlier, later):
    return (earlier[0] + later[0], earlier[1] + later[1])


def body(hidden_in, projection):
    length = hidden_in.shape[1]
    gathered = lax.all_gather(hidden_in, "row", axis=0, tiled=True)
    flat_rows = gathered.reshape(-1, gathered.shape[2])
    partial_sums = jnp.dot(
        flat_rows,
        lax.all_gather(projection, "seq", axis=0, tiled=True),
        preferred_element_type=jnp.float32,
    )
    partial_sums = partial_sums.reshape(gathered.shape[0], length, -1)
    projected = lax.psum_scatter(
        partial_sums.astype(jnp.bfloat16), "col", scatter_dimension=0, tiled=True
    )
    seqs_here = projected.shape[0]
    projected = projected.reshape(seqs_here, length, -1, 3, HD)
    total_len = lax.axis_size("seq") * length
    positions = (lax.axis_index("seq") * length + jnp.arange(length, dtype=jnp.int32)).astype(
        jnp.float32
    )
    angle = positions * (0.5 * math.pi / total_len)
    query_feat = feature_map(projected[:, :, :, 0], angle, HD ** (-0.5))
    key_feat = feature_map(projected[:, :, :, 1], angle, 1.0)
    values = projected[:, :, :, 2]
    own_state = jnp.einsum("bjhf,bjhd->bhfd", key_feat, values, preferred_element_type=jnp.float32)
    own_norm = jnp.sum(key_feat.astype(jnp.float32), axis=1)
    identity = (jnp.zeros_like(own_state), jnp.zeros_like(own_norm))
    state, norm = entering((own_state, own_norm), "seq", add_pair, identity)
    causal = jnp.tril(jnp.ones((length, length), jnp.bool_))
    scores = jnp.einsum("bihf,bjhf->bhij", query_feat, key_feat, preferred_element_type=jnp.float32)
    masked = jnp.where(causal, scores, 0.0)
    weights = masked.astype(jnp.bfloat16)
    numerator = jnp.einsum("bhij,bjhd->bihd", weights, values, preferred_element_type=jnp.float32)
    query_wide = query_feat.astype(jnp.float32)
    numerator = numerator + jnp.einsum(
        "bihf,bhfd->bihd", query_wide, state, precision=lax.Precision.HIGHEST
    )
    denominator = jnp.sum(masked, axis=-1) + jnp.einsum(
        "bihf,bhf->bhi", query_wide, norm, precision=lax.Precision.HIGHEST
    )
    denominator = jnp.maximum(denominator, 1.0)
    output = (numerator / jnp.transpose(denominator, (0, 2, 1))[..., None]).astype(jnp.bfloat16)
    return output.reshape(seqs_here, length, -1)


def solution(mesh):
    placed = (P("row", "seq", "col"), P(("col", "seq"), "row"))
    return jax.shard_map(
        body, mesh=mesh, in_specs=placed, out_specs=P("col", "seq", "row"), check_vma=False
    )
```

profile of v0, /device:TPU:10, one launch (start us, length us, event | category | flops | bytes accessed | tf_op | source)
XLA Modules:
  0.0 395.1 jit_solution(11634957935822682071)
XLA Ops:
  6.5 0.0 all-gather.8.cloned.1.call-start
  6.5 0.7 all-gather.8.cloned.1.call-update
  7.3 0.0 all-gather.6.cloned.1.call-start
  7.3 0.7 all-gather.6.cloned.1.call-update
  8.0 0.0 reduce-scatter.2.cloned.1.call-start
  8.1 82.3 %all-gather.8.cloned.1.call-done = bf16[1536,1152]{1,0:T(8,128)(2,1)} async-done(((bf16[96,1152]{1,0:T(8,128)(2,1)}), bf16[1536,1152]{1,0:T(8,128)(2,1)}) %all-gather.8.cloned.1.call-update) | async-done | bytes 3538960 | tf_op jit(solution)/shard_map/all_gather | solution.py:48
  90.4 106.5 %all-gather.6.cloned.1.call-done = bf16[8,192,1536]{2,1,0:T(8,128)(2,1)} async-done(((bf16[1,192,1536]{2,1,0:T(8,128)(2,1)}), bf16[8,192,1536]{2,1,0:T(8,128)(2,1)}) %all-gather.6.cloned.1.call-update) | async-done | bytes 4718608 | tf_op jit(solution)/shard_map/all_gather | solution.py:44
  196.9 10.4 %convolution_convert_fusion = bf16[8,192,1152]{2,1,0:T(8,128)(2,1)} fusion(bf16[8,192,1536]{2,1,0:T(8,128)(2,1)} %all-gather.6.cloned.1.call-done, bf16[1536,1152]{1,0:T(8,128)(2,1)} %all-gather.8.cloned.1.call-done), kind=kOutput, calls=%fused_computation.2 | convolution fusion | flops 5437587456 | bytes 11796480 | tf_op jit(solution)/shard_map/dot_general | solution.py:46
  207.3 0.0 reduce-scatter.2.cloned.1.call-update
  207.4 0.0 all-gather.10.cloned.1.call-start
  207.4 63.0 %reduce-scatter.2.cloned.1.call-done = bf16[2,192,1152]{2,1,0:T(8,128)(2,1)} async-done(((bf16[8,192,1152]{2,1,0:T(8,128)(2,1)}), bf16[2,192,1152]{2,1,0:T(8,128)(2,1)}) %reduce-scatter.2.cloned.1.call-update) | async-done | bytes 884752 | tf_op jit(solution)/shard_map/reduce_scatter | solution.py:52
  270.4 2.1 reshape.31
  272.5 1.2 fusion.22
  273.8 0.3 fusion.6
  274.1 1.2 convolution_convert_fusion.1
  275.3 0.0 all-gather.10.cloned.1.call-update
  275.3 0.1 fusion.9
  275.4 31.0 %all-gather.1 = bf16[32,3,256]{2,1,0:T(4,128)(2,1)S(1)} all-gather(bf16[2,3,256]{2,1,0:T(4,128)(2,1)S(1)} %fusion.9), channel_id=3, replica_groups=mesh['row'=8,'col'=4,'seq'=16] {'seq'}, dimensions={0}, use_global_device_ids=true | all-gather | bytes 52224 | tf_op jit(solution)/shard_map/all_gather | solution.py:14
  306.4 1.2 fusion.23
  307.6 54.6 %all-gather.10.cloned.1.call-done = bf16[32,3,256,128]{3,2,1,0:T(8,128)(2,1)} async-done(((bf16[2,3,256,128]{3,2,1,0:T(8,128)(2,1)}), bf16[32,3,256,128]{3,2,1,0:T(8,128)(2,1)}) %all-gather.10.cloned.1.call-update) | async-done | bytes 6291472 | tf_op jit(solution)/shard_map/all_gather | solution.py:14
  362.1 23.5 %while.16 = (s32[]{:T(128)}, f32[2,3,256,128]{3,2,1,0:T(8,128)S(1)}, f32[2,3,256]{2,1,0:T(4,128)S(1)}, s32[]{:T(128)}, bf16[16,2,3,256,128]{4,3,2,1,0:T(8,128)(2...) while((s32[]{:T(128)}, f32[2,3,256,128]{3,2,1,0:T(8,128)S(1)}, ...), condition=%wide.region_3.4_spmd.clone, body=%wide.region_2.3_spmd.clone.sunk | while | flops 792580 | bytes 1981555 | solution.py:27
  362.1 1.4 add_select_fusion.4
  363.6 1.4 add_select_fusion.4
  365.1 1.4 add_select_fusion.4
  366.6 1.4 add_select_fusion.4
  368.0 1.4 add_select_fusion.4
  369.5 1.4 add_select_fusion.4
  371.0 1.4 add_select_fusion.4
  372.4 1.4 add_select_fusion.4
  373.9 1.4 add_select_fusion.4
  375.4 1.4 add_select_fusion.4
  376.9 1.4 add_select_fusion.4
  378.3 1.4 add_select_fusion.4
  379.8 1.4 add_select_fusion.4
  381.3 1.4 add_select_fusion.4
  382.7 1.4 add_select_fusion.4
  384.2 1.4 add_select_fusion.4
  385.7 0.6 fusion.12
  386.2 0.0 copy-start
  386.2 0.7 fusion.19
  387.0 0.4 copy-done
  387.3 0.5 fusion.5
  387.8 0.8 copy.35
  (21 shorter events, 0.4 us)
Async XLA Ops:
  6.5 83.9 %all-gather.8.cloned.1.call-start = ((), (), s32[]{:S(2)}) async-start(), calls=%async_computation.2 | async-start | bytes 3760128 | tf_op jit(solution)/shard_map/all_gather | solution.py:48
  7.3 189.7 %all-gather.6.cloned.1.call-start = ((), (), s32[]{:S(2)}) async-start(), calls=%async_computation.1 | async-start | bytes 5308416 | tf_op jit(solution)/shard_map/all_gather | solution.py:44
  8.0 262.4 %reduce-scatter.2.cloned.1.call-start = ((), (), s32[]{:S(2)}) async-start(), calls=%async_computation.3 | async-start | bytes 4423680 | tf_op jit(solution)/shard_map/reduce_scatter | solution.py:52
  207.4 154.8 %all-gather.10.cloned.1.call-start = ((), (), s32[]{:S(2)}) async-start(), calls=%async_computation.4 | async-start | bytes 6684672 | tf_op jit(solution)/shard_map/all_gather | solution.py:14
  386.2 1.1 copy-start
Sparse Core Ops, SparseCore 0:
  9.4 80.9 all-gather.7
  92.5 104.3 all-gather.5
  207.5 62.9 reduce-scatter.1
  275.4 86.6 all-gather.9
where the time goes:
time: 396 us; the launch traced here: 395 us
  waiting for transfers between devices  308 us (78%)
  blocking collectives  31 us (8%)
  other arithmetic  23.6 us (6%)
  matrix products  14.5 us (4%)
  between operations  13.2 us (3%)
  local copies, waits for them, and re-layouts  4.46 us (1%)
    all_gather x1, waiting for transfers between devices, body(): gathered = lax.all_gather(hidden_in, 'row', axis=0, tiled=True)  107 us
    all_gather x1, waiting for transfers between devices, body(): lax.all_gather(projection, 'seq', axis=0, tiled=True)  82.3 us
    reduce_scatter x1, waiting for transfers between devices, body(): lax.psum_scatter(partial_sums.astype(jnp.bfloat16), 'col', scatter_dimens...  63 us
    all_gather x1, waiting for transfers between devices, entering(): lax.all_gather(part.astype(kind), axis)  54.6 us
    all_gather x1, blocking collectives, entering(): lax.all_gather(part.astype(kind), axis)  31 us
    select_n x32, other arithmetic, turn(): return jax.tree.map(lambda a, b: jnp.where(reached, a, b), new, before)  23.1 us
    dot_general x1, matrix products, body(): jnp.dot(flat_rows, lax.all_gather(projection, 'seq', axis=0, tiled=True),...  10.4 us
  transfers between devices with their start and end apart: 4, of which 4 were waited for; matrix products, arithmetic and copies ran while one was open for 0% of the time, Pallas kernels for 0%

commit v1 on v0

v1 whole, which is shorter than its diff:
```python
import functools
import math

import jax
import jax.numpy as jnp
from jax import lax
from jax.experimental import pallas as pl
from jax.experimental.pallas import tpu as pltpu
from jax.sharding import PartitionSpec as P

HD = 128
NX = 4
CHUNK = 96
QSTART = 4
MESH = pl.DeviceIdType.MESH
BF = jnp.bfloat16
F32 = jnp.float32


def dot(a, b, dims=((1,), (0,))):
    return lax.dot_general(a, b, (dims, ((), ())), preferred_element_type=F32)


def kernel(
    nseq, hid, proj, cos_ref, sin_ref, out,
    a_buf, wkv, wq, acc_f, acc_h, cs_kv, cs_q, cr_kv, cr_q, ys_kv, ys_q, yr_kv, yr_q,
    pkv, kf_buf, vx_buf, qf_buf, nd_buf, own, rb, ob,
    loc, y_s, y_r, x_s, x_r, z_s, z_r, c_s, c_r, h_s, h_r, p_s, p_r,
):
    length = hid.shape[1]
    half = length // 2
    shard = proj.shape[0]
    zhalf = shard // 2
    heads = proj.shape[1] // (3 * HD)
    r = lax.axis_index("row")
    c = lax.axis_index("col")
    z = lax.axis_index("seq")
    x, yl = r // 2, r % 2
    yh, core = c // 2, c % 2
    right = lax.rem(x + 1, NX) * 2 + yl
    left = lax.rem(x + NX - 1, NX) * 2 + yl
    ypart = x * 2 + (1 - yl)
    up = lax.rem(z + 1, nseq)
    down = lax.rem(z + nseq - 1, nseq)
    c1 = 2 * yh + (1 - core)
    c2 = 2 * (1 - yh) + core
    c3 = 2 * (1 - yh) + (1 - core)

    loads = [pltpu.make_async_copy(hid.at[0], a_buf.at[0, yl], loc.at[0])]
    mine = pl.ds(pl.multiple_of(z * shard, shard), shard)
    for h in range(heads):
        loads.append(pltpu.make_async_copy(
            proj.at[:, (3 * h + 1) * HD:(3 * h + 3) * HD], wkv.at[mine, 2 * h * HD:2 * (h + 1) * HD], loc.at[1 + 2 * h]))
        loads.append(pltpu.make_async_copy(
            proj.at[:, 3 * h * HD:(3 * h + 1) * HD], wq.at[mine, h * HD:(h + 1) * HD], loc.at[2 + 2 * h]))
    for ld in loads:
        ld.start()

    barrier = pltpu.get_barrier_semaphore()
    peers = [{"row": right}, {"row": left}, {"row": ypart}, {"seq": up}, {"seq": down}, {"col": c1}, {"col": c2}]
    for peer in peers:
        pl.semaphore_signal(barrier, inc=1, device_id=peer, device_id_type=MESH)
    for ld in loads:
        ld.wait()
    pl.semaphore_wait(barrier, len(peers))

    sent = []

    def send(src, dst, s_sem, r_sem, peer):
        cp = pltpu.make_async_remote_copy(src_ref=src, dst_ref=dst, send_sem=s_sem, recv_sem=r_sem,
                                          device_id=peer, device_id_type=MESH)
        cp.start()
        sent.append(cp)
        return cp

    rows_a, rows_b = slice(0, half), slice(half, length)
    yp = {"row": ypart}
    rt = {"row": right}
    lf = {"row": left}

    def z_src(way, step):
        owner = lax.rem(z + nseq - (step - 1), nseq) if way == 0 else lax.rem(z + step - 1, nseq)
        return owner * shard

    def z_ref(buf, way, step, part):
        return buf.at[pl.ds(pl.multiple_of(z_src(way, step) + part * zhalf, zhalf), zhalf)]

    last = nseq // 2
    z_copies = {}

    def z_used(way, step, part):
        return step < last or part == way

    def z_send(kind, step):
        buf = (wkv, wq)[kind]
        for part in range(2):
            for way in range(2):
                if z_used(way, step, part):
                    ref = z_ref(buf, way, step, part)
                    k = (kind, step - 1, way, part)
                    z_copies[k] = send(ref, ref, z_s.at[k], z_r.at[k], {"seq": up if way == 0 else down})

    def z_step(kind, step):
        buf = (wkv, wq)[kind]
        for part in range(2):
            for way in range(2):
                if z_used(way, step, part):
                    z_copies[(kind, step - 1, way, part)].wait_recv()
                    if step < last and z_used(way, step + 1, part):
                        ref = z_ref(buf, way, step + 1, part)
                        k = (kind, step, way, part)
                        z_copies[k] = send(ref, ref, z_s.at[k], z_r.at[k], {"seq": up if way == 0 else down})

    yl1 = 1 - yl
    z_send(0, 1)
    y0 = send(a_buf.at[0, yl, rows_a], a_buf.at[0, yl, rows_a], y_s.at[0], y_r.at[0], yp)
    r0 = send(a_buf.at[0, yl, rows_a], a_buf.at[3, yl, rows_a], x_s.at[0], x_r.at[0], rt)
    l0 = send(a_buf.at[0, yl, rows_b], a_buf.at[1, yl, rows_b], x_s.at[1], x_r.at[1], lf)
    y1 = send(a_buf.at[0, yl, rows_b], a_buf.at[0, yl, rows_b], y_s.at[1], y_r.at[1], yp)
    r1 = send(a_buf.at[0, yl, rows_b], a_buf.at[3, yl, rows_b], x_s.at[2], x_r.at[2], rt)
    l1 = send(a_buf.at[0, yl, rows_a], a_buf.at[1, yl, rows_a], x_s.at[3], x_r.at[3], lf)
    late = [r1, l1]
    for step in range(1, last + 1):
        z_step(0, step)
        if step == QSTART:
            z_send(1, 1)
        if step > QSTART:
            z_step(1, step - QSTART)
        if step == 2:
            r0.wait_recv()
            rf = send(a_buf.at[3, yl, rows_a], a_buf.at[2, yl, rows_a], x_s.at[4], x_r.at[4], rt)
            l0.wait_recv()
            lfw = send(a_buf.at[1, yl, rows_b], a_buf.at[2, yl, rows_b], x_s.at[5], x_r.at[5], lf)
        if step == 4:
            y0.wait_recv()
            y1.wait_recv()
            late.append(send(a_buf.at[0, yl1], a_buf.at[3, yl1], x_s.at[6], x_r.at[6], rt))
            late.append(send(a_buf.at[0, yl1], a_buf.at[1, yl1], x_s.at[7], x_r.at[7], lf))
        if step == 6:
            rf.wait_recv()
            late.append(send(a_buf.at[2, yl, rows_a], a_buf.at[2, yl, rows_a], y_s.at[2], y_r.at[2], yp))
            lfw.wait_recv()
            late.append(send(a_buf.at[2, yl, rows_b], a_buf.at[2, yl, rows_b], y_s.at[3], y_r.at[3], yp))
    q_next = last - QSTART + 1

    z_step(1, q_next)
    for cp in late:
        cp.wait_recv()
    z_step(1, q_next + 1)

    depth = a_buf.shape[3]

    def part_of(owner, w):
        j = lax.rem(owner + NX - x, NX)
        return dot(a_buf[j].reshape(2 * length, depth), w[...])

    core_peer = {"col": c1}
    far_peer = {"col": c2}

    def reduce_start(w, cs, cr, ys, yr, af, ah, k, between):
        cs[0] = part_of(c3, w).astype(BF)
        g0 = send(cs.at[0], cr.at[0], c_s.at[k, 0], c_r.at[k, 0], core_peer)
        af[...] = part_of(c2, w)
        between()
        g0.wait_recv()
        ys[...] = (af[...] + cr[0].astype(F32)).astype(BF)
        far = send(ys, yr, h_s.at[k], h_r.at[k], far_peer)
        cs[1] = part_of(c1, w).astype(BF)
        g1 = send(cs.at[1], cr.at[1], c_s.at[k, 1], c_r.at[k, 1], core_peer)
        ah[...] = part_of(c, w)
        return g1, far

    nkv = 2 * heads * HD
    acc_fk, acc_hk = acc_f.at[:, :nkv], acc_h.at[:, :nkv]
    acc_fq, acc_hq = acc_f.at[:, nkv:], acc_h.at[:, nkv:]
    g1, far = reduce_start(wkv, cs_kv, cr_kv, ys_kv, yr_kv, acc_fk, acc_hk, 0, lambda: z_step(1, q_next + 2))
    z_step(1, q_next + 3)
    g1q, farq = reduce_start(wq, cs_q, cr_q, ys_q, yr_q, acc_fq, acc_hq, 1, lambda: None)
    g1.wait_recv()
    far.wait_recv()
    pkv[...] = (acc_hk[...] + cr_kv[1].astype(F32) + yr_kv[...].astype(F32)).astype(BF)

    cosine, sine = cos_ref[...], sin_ref[...]
    ones8 = jnp.ones((8, length), BF)
    pairs = [(b, h) for b in range(2) for h in range(heads)]
    norms = len(pairs) * 2 * HD
    for i, (b, h) in enumerate(pairs):
        rows = slice(b * length, (b + 1) * length)
        key = jnp.maximum(pkv[rows, 2 * h * HD:(2 * h + 1) * HD].astype(F32), 0.0)
        val = pkv[rows, (2 * h + 1) * HD:(2 * h + 2) * HD]
        kc, ks = (key * cosine).astype(BF), (key * sine).astype(BF)
        kf_buf[i, :, :HD] = kc
        kf_buf[i, :, HD:] = ks
        vx_buf[i, :, :HD] = val
        vx_buf[i, :, HD:] = jnp.ones((length, HD), BF)
        at = i * 2 * HD
        own[at:at + HD] = dot(kc, val, ((0,), (0,)))
        own[at + HD:at + 2 * HD] = dot(ks, val, ((0,), (0,)))
        own[norms + 16 * i:norms + 16 * i + 8] = dot(ones8, kc)
        own[norms + 16 * i + 8:norms + 16 * i + 16] = dot(ones8, ks)

    def pass_on(i):
        rows = pl.ds(pl.multiple_of(i * CHUNK, CHUNK), CHUNK)
        return rows, pltpu.make_async_remote_copy(
            src_ref=ob.at[rows], dst_ref=rb.at[rows], send_sem=p_s.at[i], recv_sem=p_r.at[i],
            device_id={"seq": up}, device_id_type=MESH)

    chunks = rb.shape[0] // CHUNK

    def chain():
        @pl.loop(0, chunks)
        def _(i):
            rows, cp = pass_on(i)

            @pl.when(z > 0)
            def _():
                cp.wait_recv()

            @pl.when(z == 0)
            def _():
                rb[rows] = jnp.zeros((CHUNK, HD), BF)

            @pl.when(z < nseq - 1)
            def _():
                ob[rows] = (rb[rows].astype(F32) + own[rows]).astype(BF)
                cp.start()

    early = 4

    @pl.when(z < early)
    def _():
        chain()

    g1q.wait_recv()
    farq.wait_recv()
    acc_hq[...] = acc_hq[...] + cr_q[1].astype(F32) + yr_q[...].astype(F32)
    ii = lax.broadcasted_iota(jnp.int32, (length, length), 0)
    jj = lax.broadcasted_iota(jnp.int32, (length, length), 1)
    causal = jj <= ii
    for i, (b, h) in enumerate(pairs):
        rows = slice(b * length, (b + 1) * length)
        q = acc_hq[rows, h * HD:(h + 1) * HD].astype(BF).astype(F32)
        q = jnp.maximum(q, 0.0)
        qf_buf[i, :, :HD] = (q * cosine * HD ** -0.5).astype(BF)
        qf_buf[i, :, HD:] = (q * sine * HD ** -0.5).astype(BF)
        s = dot(qf_buf[i], kf_buf[i], ((1,), (1,)))
        wts = jnp.where(causal, s, 0.0).astype(BF)
        nd_buf[i] = dot(wts, vx_buf[i])

    @pl.when(z >= early)
    def _():
        chain()

    for i, (b, h) in enumerate(pairs):
        at = i * 2 * HD
        qf = qf_buf[i]
        num = nd_buf[i, :, :HD] + dot(qf, rb[at:at + 2 * HD])
        nc = rb[norms + 16 * i:norms + 16 * i + 16].astype(F32)
        nrm = jnp.concatenate(
            [jnp.broadcast_to(nc[0:1], (HD, HD)), jnp.broadcast_to(nc[8:9], (HD, HD))], axis=1).astype(BF)
        den = nd_buf[i, :, HD:] + dot(qf, nrm, ((1,), (1,)))
        out[b, :, h * HD:(h + 1) * HD] = (num / jnp.maximum(den, 1.0)).astype(BF)

    for cp in sent:
        cp.wait_send()

    @pl.when(z < nseq - 1)
    def _():
        @pl.loop(0, chunks)
        def _(i):
            pass_on(i)[1].wait_send()


def body(nseq, hidden_in, projection):
    length, depth = hidden_in.shape[1:]
    shard, width = projection.shape
    heads = width // (3 * HD)
    positions = (lax.axis_index("seq") * length + jnp.arange(length, dtype=jnp.int32)).astype(F32)
    angle = positions * (0.5 * math.pi / (nseq * length))
    cosine = jnp.broadcast_to(jnp.cos(angle)[:, None], (length, HD))
    sine = jnp.broadcast_to(jnp.sin(angle)[:, None], (length, HD))
    nkv, nq = 2 * heads * HD, heads * HD
    rows = 2 * length
    pairs = 2 * heads
    st = pairs * (2 * HD + 16)
    vm, dma = pltpu.VMEM, pltpu.SemaphoreType.DMA
    anywhere = pl.BlockSpec(memory_space=pl.ANY)
    vmem = pl.BlockSpec(memory_space=pltpu.VMEM)
    zsem = (2, nseq // 2, 2, 2)
    return pl.pallas_call(
        functools.partial(kernel, nseq),
        out_shape=jax.ShapeDtypeStruct((2, length, nq), BF),
        in_specs=[anywhere, anywhere, vmem, vmem],
        out_specs=vmem,
        scratch_shapes=[
            vm((NX, 2, length, depth), BF), vm((nseq * shard, nkv), BF), vm((nseq * shard, nq), BF),
            vm((rows, width), F32), vm((rows, width), F32),
            vm((2, rows, nkv), BF), vm((2, rows, nq), BF), vm((2, rows, nkv), BF), vm((2, rows, nq), BF),
            vm((rows, nkv), BF), vm((rows, nq), BF), vm((rows, nkv), BF), vm((rows, nq), BF),
            vm((rows, nkv), BF),
            vm((pairs, length, 2 * HD), BF), vm((pairs, length, 2 * HD), BF), vm((pairs, length, 2 * HD), BF),
            vm((pairs, length, 2 * HD), F32),
            vm((st, HD), F32), vm((st, HD), BF), vm((st, HD), BF),
            dma((1 + 2 * heads,)), dma((4,)), dma((4,)), dma((8,)), dma((8,)),
            dma(zsem), dma(zsem), dma((2, 2)), dma((2, 2)), dma((2,)), dma((2,)),
            dma((st // CHUNK,)), dma((st // CHUNK,)),
        ],
        compiler_params=pltpu.CompilerParams(
            collective_id=0, has_side_effects=True, vmem_limit_bytes=56 * 1024 * 1024),
    )(hidden_in, projection, cosine, sine)


def solution(mesh):
    placed = (P("row", "seq", "col"), P(("col", "seq"), "row"))
    return jax.shard_map(
        functools.partial(body, mesh.shape["seq"]), mesh=mesh, in_specs=placed,
        out_specs=P("col", "seq", "row"), check_vma=False)
```

time: 396 us -> 127 us (0.32)
  the two profiles are of different devices: /device:TPU:10 before, /device:TPU:480 now
where the time goes in v1:
time: 127 us
  Pallas kernels  124 us (98%)
  local copies, waits for them, and re-layouts  3.18 us (3%)
    pallas_call x1, Pallas kernels, body(): pl.pallas_call(functools.partial(kernel, nseq), out_shape=jax.ShapeDtypeS...  124 us

profile of v1, /device:TPU:480, one launch (start us, length us, event | category | flops | bytes accessed | tf_op | source)
XLA Modules:
  0.0 126.8 jit_solution(7790509575743792229)
XLA Ops:
  0.0 0.7 broadcast_in_dim.5.sin_ref
  0.8 0.7 broadcast_in_dim.4.cos_ref
  1.5 123.5 %shard_map.28 = bf16[2,192,384]{2,1,0:T(8,128)(2,1)} custom-call(bf16[1,192,1536]{2,1,0:T(8,128)(2,1)} %hid.1, bf16[96,1152]{1,0:T(8,128)(2,1)} %proj.1, f32[192,128]{1,0:T(8,128)} %broadcast_in_dim.4.cos_ref, f32[192,128]{1,0:T(8,128)} %broadcast_in_dim.5.sin_ref), custom_call_target="tpu_custom_call" | custom-call | tf_op jit(solution)/shard_map/pallas_call | solution.py:290
  125.1 1.7 %copy.4 = bf16[2,192,384]{2,1,0:T(8,128)(2,1)} copy(bf16[2,192,384]{2,1,0:T(8,128)(2,1)} %shard_map.28) | data formatting | bytes 589824
  (1 shorter events, 0.0 us)

commit v2 on v1

v2 whole, which is shorter than its diff:
```python
import functools
import math

import jax
import jax.numpy as jnp
from jax import lax
from jax.experimental import pallas as pl
from jax.experimental.pallas import tpu as pltpu
from jax.sharding import PartitionSpec as P

HD = 128
NX = 4
CHUNK = 96
NORM = 16
QSTART = 5
EARLY = 8
PIECES = (6, 6)
MESH = pl.DeviceIdType.MESH
BF = jnp.bfloat16
F32 = jnp.float32


def dot(a, b, dims=((1,), (0,))):
    return lax.dot_general(a, b, (dims, ((), ())), preferred_element_type=F32)


def kernel(
    nseq, hid, proj, out,
    a_buf, wkv, wq, acc_k, acc_q, cs_kv, cs_q, cr_kv, cr_q, ys_kv, ys_q, yr_kv, yr_q,
    trig, pkv, kf_buf, vx_buf, qf_buf, nd_buf, own, own0, rb, rb0, ob,
    loc, y_s, y_r, x_s, x_r, k_s, k_r, q_s, q_r, c_s, c_r, h_s, h_r, p_s, p_r, o_s, o_r, f_s, f_r,
):
    length = hid.shape[1]
    half = length // 2
    shard = proj.shape[0]
    heads = proj.shape[1] // (3 * HD)
    pairs = 2 * heads
    r = lax.axis_index("row")
    c = lax.axis_index("col")
    z = lax.axis_index("seq")
    x, yl = r // 2, r % 2
    yh, core = c // 2, c % 2
    right = lax.rem(x + 1, NX) * 2 + yl
    left = lax.rem(x + NX - 1, NX) * 2 + yl
    ypart = x * 2 + (1 - yl)
    up = lax.rem(z + 1, nseq)
    down = lax.rem(z + nseq - 1, nseq)
    c1 = 2 * yh + (1 - core)
    c2 = 2 * (1 - yh) + core
    c3 = 2 * (1 - yh) + (1 - core)

    loads = [pltpu.make_async_copy(hid.at[0], a_buf.at[0, yl], loc.at[0])]
    mine = pl.ds(pl.multiple_of(z * shard, shard), shard)
    for h in range(heads):
        loads.append(pltpu.make_async_copy(
            proj.at[:, (3 * h + 1) * HD:(3 * h + 3) * HD], wkv.at[mine, 2 * h * HD:2 * (h + 1) * HD], loc.at[1 + 2 * h]))
        loads.append(pltpu.make_async_copy(
            proj.at[:, 3 * h * HD:(3 * h + 1) * HD], wq.at[mine, h * HD:(h + 1) * HD], loc.at[2 + 2 * h]))
    for ld in loads:
        ld.start()

    barrier = pltpu.get_barrier_semaphore()
    peers = [{"row": right}, {"row": left}, {"row": ypart}, {"seq": up}, {"seq": down}, {"col": c1}, {"col": c2}]
    for peer in peers:
        pl.semaphore_signal(barrier, inc=1, device_id=peer, device_id_type=MESH)
    for ld in loads:
        ld.wait()
    pl.semaphore_wait(barrier, len(peers))

    sent = []

    def remote(src, dst, s_sem, r_sem, peer):
        return pltpu.make_async_remote_copy(src_ref=src, dst_ref=dst, send_sem=s_sem, recv_sem=r_sem,
                                            device_id=peer, device_id_type=MESH)

    def send(*what):
        cp = remote(*what)
        cp.start()
        sent.append(cp)
        return cp

    rows_a, rows_b = slice(0, half), slice(half, length)
    yp = {"row": ypart}
    rt = {"row": right}
    lf = {"row": left}

    last = nseq // 2
    z_copies = {}

    def z_used(kind, way, step, part):
        return step < last or (part < PIECES[kind] // 2) == (way == 0)

    def z_one(kind, way, step, part):
        size = shard // PIECES[kind]
        owner = lax.rem(z + nseq - (step - 1), nseq) if way == 0 else lax.rem(z + step - 1, nseq)
        ref = (wkv, wq)[kind].at[pl.ds(pl.multiple_of(owner * shard + part * size, size), size)]
        k = (step - 1, way, part)
        z_copies[(kind,) + k] = send(
            ref, ref, (k_s, q_s)[kind].at[k], (k_r, q_r)[kind].at[k], {"seq": up if way == 0 else down})

    def z_send(kind):
        for part in range(PIECES[kind]):
            for way in range(2):
                z_one(kind, way, 1, part)

    def z_step(kind, step):
        for part in range(PIECES[kind]):
            for way in range(2):
                if z_used(kind, way, step, part):
                    z_copies[(kind, step - 1, way, part)].wait_recv()
                    if step < last and z_used(kind, way, step + 1, part):
                        z_one(kind, way, step + 1, part)

    yl1 = 1 - yl
    z_send(0)
    y0 = send(a_buf.at[0, yl, rows_a], a_buf.at[0, yl, rows_a], y_s.at[0], y_r.at[0], yp)
    r0 = send(a_buf.at[0, yl, rows_a], a_buf.at[3, yl, rows_a], x_s.at[0], x_r.at[0], rt)
    l0 = send(a_buf.at[0, yl, rows_b], a_buf.at[1, yl, rows_b], x_s.at[1], x_r.at[1], lf)
    y1 = send(a_buf.at[0, yl, rows_b], a_buf.at[0, yl, rows_b], y_s.at[1], y_r.at[1], yp)
    r1 = send(a_buf.at[0, yl, rows_b], a_buf.at[3, yl, rows_b], x_s.at[2], x_r.at[2], rt)
    l1 = send(a_buf.at[0, yl, rows_a], a_buf.at[1, yl, rows_a], x_s.at[3], x_r.at[3], lf)
    late = []

    place = (z * length + lax.broadcasted_iota(jnp.int32, (length, HD), 0)).astype(F32)
    angle = place * (0.5 * math.pi / (nseq * length))
    trig[0] = jnp.cos(angle)
    trig[1] = jnp.sin(angle)

    for step in range(1, last + 1):
        z_step(0, step)
        if step == QSTART:
            z_send(1)
        if step > QSTART:
            z_step(1, step - QSTART)
        if step == 2:
            r0.wait_recv()
            rf = send(a_buf.at[3, yl, rows_a], a_buf.at[2, yl, rows_a], x_s.at[4], x_r.at[4], rt)
            l0.wait_recv()
            lfw = send(a_buf.at[1, yl, rows_b], a_buf.at[2, yl, rows_b], x_s.at[5], x_r.at[5], lf)
        if step == 4:
            y0.wait_recv()
            y1.wait_recv()
            late.append(send(a_buf.at[0, yl1], a_buf.at[3, yl1], x_s.at[6], x_r.at[6], rt))
            late.append(send(a_buf.at[0, yl1], a_buf.at[1, yl1], x_s.at[7], x_r.at[7], lf))
        if step == 6:
            rf.wait_recv()
            late.append(send(a_buf.at[2, yl, rows_a], a_buf.at[2, yl, rows_a], y_s.at[2], y_r.at[2], yp))
            lfw.wait_recv()
            late.append(send(a_buf.at[2, yl, rows_b], a_buf.at[2, yl, rows_b], y_s.at[3], y_r.at[3], yp))
    q_steps = list(range(last - QSTART + 1, last + 1))

    def q_step():
        if q_steps:
            z_step(1, q_steps.pop(0))

    r1.wait_recv()
    l1.wait_recv()

    def part_of(owner, yb, w):
        return dot(a_buf[lax.rem(owner + NX - x, NX), yb], w[...])

    core_peer = {"col": c1}
    far_peer = {"col": c2}
    halves = (yl, yl1)

    def reduce_far(t, k, w, cs, cr, ys, yr, between):
        cs[t, 0] = part_of(c3, halves[t], w).astype(BF)
        near = send(cs.at[t, 0], cr.at[t, 0], c_s.at[k, t, 0], c_r.at[k, t, 0], core_peer)
        total = part_of(c2, halves[t], w)
        between()
        near.wait_recv()
        ys[t] = (total + cr[t, 0].astype(F32)).astype(BF)
        return send(ys.at[t], yr.at[t], h_s.at[k, t], h_r.at[k, t], far_peer)

    def reduce_near(t, k, w, cs, cr, acc):
        cs[t, 1] = part_of(c1, halves[t], w).astype(BF)
        near = send(cs.at[t, 1], cr.at[t, 1], c_s.at[k, t, 1], c_r.at[k, t, 1], core_peer)
        acc[t] = part_of(c, halves[t], w)
        return near

    nothing = lambda: None
    kv_far, kv_near, q_far, q_near = [], [], [], []
    kv_far.append(reduce_far(0, 0, wkv, cs_kv, cr_kv, ys_kv, yr_kv, nothing))
    q_step()
    kv_near.append(reduce_near(0, 0, wkv, cs_kv, cr_kv, acc_k))
    q_step()
    for cp in late:
        cp.wait_recv()
    kv_far.append(reduce_far(1, 0, wkv, cs_kv, cr_kv, ys_kv, yr_kv, q_step))
    kv_near.append(reduce_near(1, 0, wkv, cs_kv, cr_kv, acc_k))
    while q_steps:
        q_step()

    block = 2 * HD + 2 * NORM
    ones = jnp.ones((NORM, length), BF)

    def states(t):
        kv_near[t].wait_recv()
        kv_far[t].wait_recv()
        yb = halves[t]
        pkv[t] = (acc_k[t] + cr_kv[t, 1].astype(F32) + yr_kv[t].astype(F32)).astype(BF)
        cosine, sine = trig[0], trig[1]
        for h in range(heads):
            i = yb * heads + h
            key = jnp.maximum(pkv[t, :, 2 * h * HD:(2 * h + 1) * HD].astype(F32), 0.0)
            val = pkv[t, :, (2 * h + 1) * HD:(2 * h + 2) * HD]
            kc, ks = (key * cosine).astype(BF), (key * sine).astype(BF)
            kf_buf[i, :, :HD] = kc
            kf_buf[i, :, HD:] = ks
            vx_buf[i, :, :HD] = val
            vx_buf[i, :, HD:] = jnp.ones((length, HD), BF)
            own[i, :HD] = dot(kc, val, ((0,), (0,)))
            own[i, HD:2 * HD] = dot(ks, val, ((0,), (0,)))
            own[i, 2 * HD:2 * HD + NORM] = dot(ones, kc)
            own[i, 2 * HD + NORM:] = dot(ones, ks)

    states(0)
    states(1)

    per = block // CHUNK
    give = remote(own, own0, o_s.at[0], o_r.at[0], core_peer)

    @pl.when(core == 0)
    def _():
        give.start()

    def rows_of(k):
        return pl.ds(pl.multiple_of(k * CHUNK, CHUNK), CHUNK)

    def hop(s, i, k):
        return remote(ob.at[s, i, rows_of(k)], (rb, rb0)[s].at[i, rows_of(k)], p_s.at[s, i, k], p_r.at[s, i, k], {"seq": up})

    def hand(i, k):
        return remote(rb0.at[i, rows_of(k)], rb.at[i, rows_of(k)], f_s.at[i, k], f_r.at[i, k], core_peer)

    def final(i):
        b, h = i // heads, lax.rem(i, heads)
        qf = qf_buf[i]
        num = nd_buf[i, :, :HD] + dot(qf, rb[i, :2 * HD])
        tail = rb[i, 2 * HD:].astype(F32)
        nrm = jnp.concatenate(
            [jnp.broadcast_to(tail[0:1], (HD, HD)), jnp.broadcast_to(tail[NORM:NORM + 1], (HD, HD))], axis=1).astype(BF)
        den = nd_buf[i, :, HD:] + dot(qf, nrm, ((1,), (1,)))
        out[b, :, pl.ds(pl.multiple_of(h * HD, HD), HD)] = (num / jnp.maximum(den, 1.0)).astype(BF)

    def link(s, i):
        into, mine_s = ((rb, own), (rb0, own0))[s]

        @pl.loop(0, per)
        def _(k):
            rows = rows_of(k)

            @pl.when(z == 0)
            def _():
                ob[s, i, rows] = mine_s[i, rows].astype(BF)
                hop(s, i, k).start()

            @pl.when(z > 0)
            def _():
                hop(s, i, k).wait_recv()

                @pl.when(z < nseq - 1)
                def _():
                    ob[s, i, rows] = (into[i, rows].astype(F32) + mine_s[i, rows]).astype(BF)
                    hop(s, i, k).start()

                if s == 1:
                    hand(i, k).start()

    def chain():
        @pl.when(core == 1)
        def _():
            @pl.loop(0, pairs)
            def _(i):
                link(0, i)

            give.wait_recv()

            @pl.loop(0, pairs)
            def _(i):
                link(1, i)

                @pl.when(z == nseq - 1)
                def _():
                    final(i)

    @pl.when(z == 0)
    def _():
        rb[...] = jnp.zeros(rb.shape, BF)

    @pl.when(z < EARLY)
    def _():
        chain()

    for t in range(2):
        q_far.append(reduce_far(t, 1, wq, cs_q, cr_q, ys_q, yr_q, nothing))
    for t in range(2):
        q_near.append(reduce_near(t, 1, wq, cs_q, cr_q, acc_q))
    ii = lax.broadcasted_iota(jnp.int32, (length, length), 0)
    jj = lax.broadcasted_iota(jnp.int32, (length, length), 1)
    causal = jj <= ii
    for t in range(2):
        q_near[t].wait_recv()
        q_far[t].wait_recv()
        for h in range(heads):
            i = halves[t] * heads + h
            cols = slice(h * HD, (h + 1) * HD)
            q = acc_q[t, :, cols] + cr_q[t, 1, :, cols].astype(F32) + yr_q[t, :, cols].astype(F32)
            q = jnp.maximum(q.astype(BF).astype(F32), 0.0)
            qf_buf[i, :, :HD] = (q * trig[0] * HD ** -0.5).astype(BF)
            qf_buf[i, :, HD:] = (q * trig[1] * HD ** -0.5).astype(BF)
            s = dot(qf_buf[i], kf_buf[i], ((1,), (1,)))
            wts = jnp.where(causal, s, 0.0).astype(BF)
            nd_buf[i] = dot(wts, vx_buf[i])

    @pl.when(z >= EARLY)
    def _():
        chain()

    @pl.when((core == 0) | (z < nseq - 1))
    def _():
        @pl.loop(0, pairs)
        def _(i):
            @pl.when((core == 0) & (z > 0))
            def _():
                @pl.loop(0, per)
                def _(k):
                    hand(i, k).wait_recv()

            final(i)

    for cp in sent:
        cp.wait_send()

    @pl.when(core == 0)
    def _():
        give.wait_send()

    @pl.when(core == 1)
    def _():
        @pl.loop(0, pairs)
        def _(i):
            @pl.loop(0, per)
            def _(k):
                @pl.when(z < nseq - 1)
                def _():
                    hop(0, i, k).wait_send()
                    hop(1, i, k).wait_send()

                @pl.when(z > 0)
                def _():
                    hand(i, k).wait_send()


def body(nseq, hidden_in, projection):
    length, depth = hidden_in.shape[1:]
    shard, width = projection.shape
    heads = width // (3 * HD)
    nkv, nq = 2 * heads * HD, heads * HD
    pairs = 2 * heads
    block = 2 * HD + 2 * NORM
    vm, dma = pltpu.VMEM, pltpu.SemaphoreType.DMA
    anywhere = pl.BlockSpec(memory_space=pl.ANY)
    per = block // CHUNK
    wide = (pairs, length, 2 * HD)
    return pl.pallas_call(
        functools.partial(kernel, nseq),
        out_shape=jax.ShapeDtypeStruct((2, length, nq), BF),
        in_specs=[anywhere, anywhere],
        out_specs=pl.BlockSpec(memory_space=pltpu.VMEM),
        scratch_shapes=[
            vm((NX, 2, length, depth), BF), vm((nseq * shard, nkv), BF), vm((nseq * shard, nq), BF),
            vm((2, length, nkv), F32), vm((2, length, nq), F32),
            vm((2, 2, length, nkv), BF), vm((2, 2, length, nq), BF), vm((2, 2, length, nkv), BF), vm((2, 2, length, nq), BF),
            vm((2, length, nkv), BF), vm((2, length, nq), BF), vm((2, length, nkv), BF), vm((2, length, nq), BF),
            vm((2, length, HD), F32), vm((2, length, nkv), BF),
            vm(wide, BF), vm(wide, BF), vm(wide, BF), vm(wide, F32),
            vm((pairs, block, HD), F32), vm((pairs, block, HD), F32),
            vm((pairs, block, HD), BF), vm((pairs, block, HD), BF), vm((2, pairs, block, HD), BF),
            dma((1 + 2 * heads,)), dma((4,)), dma((4,)), dma((8,)), dma((8,)),
            dma((nseq // 2, 2, PIECES[0])), dma((nseq // 2, 2, PIECES[0])),
            dma((nseq // 2, 2, PIECES[1])), dma((nseq // 2, 2, PIECES[1])),
            dma((2, 2, 2)), dma((2, 2, 2)), dma((2, 2)), dma((2, 2)),
            dma((2, pairs, per)), dma((2, pairs, per)), dma((1,)), dma((1,)), dma((pairs, per)), dma((pairs, per)),
        ],
        compiler_params=pltpu.CompilerParams(
            collective_id=0, has_side_effects=True, vmem_limit_bytes=58 * 1024 * 1024),
    )(hidden_in, projection)


def solution(mesh):
    placed = (P("row", "seq", "col"), P(("col", "seq"), "row"))
    return jax.shard_map(
        functools.partial(body, mesh.shape["seq"]), mesh=mesh, in_specs=placed,
        out_specs=P("col", "seq", "row"), check_vma=False)
```

time: 127 us -> 105 us (0.83)
  Pallas kernels: 124 us -> 103 us
  local copies, waits for them, and re-layouts: 3.18 us -> 1.71 us
    pallas_call x1, Pallas kernels: 124 us -> 103 us  [body(): pl.pallas_call(functools.partial(kernel, nseq), out_shape=jax.ShapeDtypeS...]
    broadcast_in_dim x2 -> x0, local copies, waits for them, and re-layouts: 1.48 us -> none  [the longest x1 0.74 us: body(): sine = jnp.broadcast_to(jnp.sin(angle)[:, None], (length, HD))]
where the time goes in v2:
time: 105 us
  Pallas kernels  103 us (98%)
  local copies, waits for them, and re-layouts  1.71 us (2%)
    pallas_call x1, Pallas kernels, body(): pl.pallas_call(functools.partial(kernel, nseq), out_shape=jax.ShapeDtypeS...  103 us

profile of v2, /device:TPU:480, one launch (start us, length us, event | category | flops | bytes accessed | tf_op | source)
XLA Modules:
  0.0 105.1 jit_solution(13647727246850917045)
XLA Ops:
  0.0 103.4 %shard_map.28 = bf16[2,192,384]{2,1,0:T(8,128)(2,1)} custom-call(bf16[1,192,1536]{2,1,0:T(8,128)(2,1)} %hid.1, bf16[96,1152]{1,0:T(8,128)(2,1)} %proj.1), custom_call_target="tpu_custom_call" | custom-call | tf_op jit(solution)/shard_map/pallas_call | solution.py:366
  103.4 1.7 %copy.4 = bf16[2,192,384]{2,1,0:T(8,128)(2,1)} copy(bf16[2,192,384]{2,1,0:T(8,128)(2,1)} %shard_map.28) | data formatting | bytes 589824

commit v3 on v2

--- a/solution.py
+++ b/solution.py
@@ -14,7 +14,9 @@
 NORM = 16
 QSTART = 5
 EARLY = 8
-PIECES = (6, 6)
+SPLIT = 4
+MEET = 11
+PIECES = (6, 2)
 MESH = pl.DeviceIdType.MESH
 BF = jnp.bfloat16
 F32 = jnp.float32
@@ -27,7 +29,7 @@
 def kernel(
     nseq, hid, proj, out,
     a_buf, wkv, wq, acc_k, acc_q, cs_kv, cs_q, cr_kv, cr_q, ys_kv, ys_q, yr_kv, yr_q,
-    trig, pkv, kf_buf, vx_buf, qf_buf, nd_buf, own, own0, rb, rb0, ob,
+    trig, pkv, kf_buf, vx_buf, qf_buf, nd_buf, own, own0, rb, ob, fin,
     loc, y_s, y_r, x_s, x_r, k_s, k_r, q_s, q_r, c_s, c_r, h_s, h_r, p_s, p_r, o_s, o_r, f_s, f_r,
 ):
     length = hid.shape[1]
@@ -188,20 +190,16 @@
         cp.wait_recv()
     kv_far.append(reduce_far(1, 0, wkv, cs_kv, cr_kv, ys_kv, yr_kv, q_step))
     kv_near.append(reduce_near(1, 0, wkv, cs_kv, cr_kv, acc_k))
-    while q_steps:
-        q_step()
-
     block = 2 * HD + 2 * NORM
     ones = jnp.ones((NORM, length), BF)
 
     def states(t):
         kv_near[t].wait_recv()
         kv_far[t].wait_recv()
-        yb = halves[t]
         pkv[t] = (acc_k[t] + cr_kv[t, 1].astype(F32) + yr_kv[t].astype(F32)).astype(BF)
         cosine, sine = trig[0], trig[1]
         for h in range(heads):
-            i = yb * heads + h
+            i = t * heads + h
             key = jnp.maximum(pkv[t, :, 2 * h * HD:(2 * h + 1) * HD].astype(F32), 0.0)
             val = pkv[t, :, (2 * h + 1) * HD:(2 * h + 2) * HD]
             kc, ks = (key * cosine).astype(BF), (key * sine).astype(BF)
@@ -214,88 +212,153 @@
             own[i, 2 * HD:2 * HD + NORM] = dot(ones, kc)
             own[i, 2 * HD + NORM:] = dot(ones, ks)
 
-    states(0)
-    states(1)
+        @pl.when((core == 0) | (z < SPLIT))
+        def _():
+            give(t).start()
 
     per = block // CHUNK
-    give = remote(own, own0, o_s.at[0], o_r.at[0], core_peer)
-
-    @pl.when(core == 0)
-    def _():
-        give.start()
+
+    def give(t):
+        these = pl.ds(t * heads, heads)
+        return remote(own.at[these], own0.at[these], o_s.at[t], o_r.at[t], core_peer)
 
     def rows_of(k):
         return pl.ds(pl.multiple_of(k * CHUNK, CHUNK), CHUNK)
 
-    def hop(s, i, k):
-        return remote(ob.at[s, i, rows_of(k)], (rb, rb0)[s].at[i, rows_of(k)], p_s.at[s, i, k], p_r.at[s, i, k], {"seq": up})
-
-    def hand(i, k):
-        return remote(rb0.at[i, rows_of(k)], rb.at[i, rows_of(k)], f_s.at[i, k], f_r.at[i, k], core_peer)
-
-    def final(i):
-        b, h = i // heads, lax.rem(i, heads)
-        qf = qf_buf[i]
-        num = nd_buf[i, :, :HD] + dot(qf, rb[i, :2 * HD])
-        tail = rb[i, 2 * HD:].astype(F32)
-        nrm = jnp.concatenate(
-            [jnp.broadcast_to(tail[0:1], (HD, HD)), jnp.broadcast_to(tail[NORM:NORM + 1], (HD, HD))], axis=1).astype(BF)
-        den = nd_buf[i, :, HD:] + dot(qf, nrm, ((1,), (1,)))
-        out[b, :, pl.ds(pl.multiple_of(h * HD, HD), HD)] = (num / jnp.maximum(den, 1.0)).astype(BF)
-
-    def link(s, i):
-        into, mine_s = ((rb, own), (rb0, own0))[s]
-
-        @pl.loop(0, per)
-        def _(k):
-            rows = rows_of(k)
-
-            @pl.when(z == 0)
-            def _():
-                ob[s, i, rows] = mine_s[i, rows].astype(BF)
-                hop(s, i, k).start()
-
-            @pl.when(z > 0)
-            def _():
-                hop(s, i, k).wait_recv()
+    def hop(f, s, i, k, way, src):
+        rows = rows_of(k)
+        return remote(src.at[f, s, i, rows], rb.at[f, s, i, rows], p_s.at[f, s, i, k], p_r.at[f, s, i, k], {"seq": way})
+
+    def hand(f, i, k):
+        rows = rows_of(k)
+        return remote(rb.at[f, 1, i, rows], rb.at[2, 0, i, rows], f_s.at[i, k], f_r.at[i, k], core_peer)
+
+    def chunks(t, do):
+        @pl.loop(0, heads)
+        def _(h):
+            @pl.loop(0, per)
+            def _(k):
+                do(t * heads + h, k)
+
+    flow = (z >= SPLIT).astype(jnp.int32)
+    origin = (z == 0) | (z == SPLIT)
+
+    def relay(f, s, i, k, way, first):
+        rows = rows_of(k)
+        mine_s = (own, own0)[s]
+
+        @pl.when(first)
+        def _():
+            ob[f, s, i, rows] = mine_s[i, rows].astype(BF)
+
+        @pl.when(jnp.logical_not(first))
+        def _():
+            ob[f, s, i, rows] = (rb[f, s, i, rows].astype(F32) + mine_s[i, rows]).astype(BF)
+
+        hop(f, s, i, k, way, ob).start()
+
+    def first_up(t):
+        for s in range(2):
+            if s == 1:
+                give(t).wait_recv()
+
+            def do(i, k):
+                @pl.when(jnp.logical_not(origin))
+                def _():
+                    hop(flow, s, i, k, up, ob).wait_recv()
 
                 @pl.when(z < nseq - 1)
                 def _():
-                    ob[s, i, rows] = (into[i, rows].astype(F32) + mine_s[i, rows]).astype(BF)
-                    hop(s, i, k).start()
+                    relay(flow, s, i, k, up, origin)
 
                 if s == 1:
-                    hand(i, k).start()
-
-    def chain():
+                    @pl.when(((z > 0) & (z < SPLIT)) | (z > MEET))
+                    def _():
+                        hand(flow, i, k).start()
+
+            chunks(t, do)
+
+    def second_up(t):
+        for s in range(2):
+            def do(i, k):
+                hop(0, s, i, k, up, ob).wait_recv()
+
+                @pl.when(z < MEET)
+                def _():
+                    relay(0, s, i, k, up, False)
+
+                if s == 1:
+                    hand(0, i, k).start()
+
+            chunks(t, do)
+
+    def around(t):
+        for s in range(2):
+            if s == 1:
+                @pl.when(z < SPLIT)
+                def _():
+                    give(t).wait_recv()
+
+            def do(i, k):
+                @pl.when(z != SPLIT - 1)
+                def _():
+                    hop(0, s, i, k, down, ob).wait_recv()
+
+                @pl.when(z < SPLIT)
+                def _():
+                    relay(0, s, i, k, down, z == SPLIT - 1)
+
+                @pl.when(z > MEET + 1)
+                def _():
+                    hop(0, s, i, k, down, rb).start()
+
+                if s == 1:
+                    @pl.when(z > MEET)
+                    def _():
+                        hand(0, i, k).start()
+
+            chunks(t, do)
+
+    def chain(t):
         @pl.when(core == 1)
         def _():
-            @pl.loop(0, pairs)
-            def _(i):
-                link(0, i)
-
-            give.wait_recv()
-
-            @pl.loop(0, pairs)
-            def _(i):
-                link(1, i)
-
-                @pl.when(z == nseq - 1)
-                def _():
-                    final(i)
-
-    @pl.when(z == 0)
-    def _():
-        rb[...] = jnp.zeros(rb.shape, BF)
-
-    @pl.when(z < EARLY)
-    def _():
-        chain()
-
+            first_up(t)
+
+        @pl.when((core == 0) & ((z < SPLIT) | (z > MEET)))
+        def _():
+            around(t)
+
+    def chain_on():
+        @pl.when((core == 1) & (z >= SPLIT) & (z <= MEET))
+        def _():
+            second_up(0)
+            second_up(1)
+
+    while q_steps:
+        q_step()
     for t in range(2):
         q_far.append(reduce_far(t, 1, wq, cs_q, cr_q, ys_q, yr_q, nothing))
     for t in range(2):
         q_near.append(reduce_near(t, 1, wq, cs_q, cr_q, acc_q))
+
+    f1 = jnp.where(core == 0, 2, (z > MEET).astype(jnp.int32))
+    f2 = jnp.where(core == 0, 0, 2)
+
+    @pl.when(z == 0)
+    def _():
+        rb[f1, 0] = jnp.zeros(rb.shape[2:], BF)
+
+    early = jnp.where(core == 1, z < EARLY, z < SPLIT)
+    states(0)
+
+    states(1)
+
+    @pl.when(early)
+    def _():
+        chain(0)
+        chain(1)
+        chain_on()
+
     ii = lax.broadcasted_iota(jnp.int32, (length, length), 0)
     jj = lax.broadcasted_iota(jnp.int32, (length, length), 1)
     causal = jj <= ii
@@ -303,7 +366,7 @@
         q_near[t].wait_recv()
         q_far[t].wait_recv()
         for h in range(heads):
-            i = halves[t] * heads + h
+            i = t * heads + h
             cols = slice(h * HD, (h + 1) * HD)
             q = acc_q[t, :, cols] + cr_q[t, 1, :, cols].astype(F32) + yr_q[t, :, cols].astype(F32)
             q = jnp.maximum(q.astype(BF).astype(F32), 0.0)
@@ -313,43 +376,65 @@
             wts = jnp.where(causal, s, 0.0).astype(BF)
             nd_buf[i] = dot(wts, vx_buf[i])
 
-    @pl.when(z >= EARLY)
+    @pl.when(jnp.logical_not(early))
     def _():
-        chain()
-
-    @pl.when((core == 0) | (z < nseq - 1))
-    def _():
-        @pl.loop(0, pairs)
-        def _(i):
-            @pl.when((core == 0) & (z > 0))
-            def _():
-                @pl.loop(0, per)
-                def _(k):
-                    hand(i, k).wait_recv()
-
-            final(i)
+        chain(0)
+        chain(1)
+        chain_on()
+
+    @pl.loop(0, pairs)
+    def _(i):
+        @pl.when(((core == 0) & (z > 0)) | (z > MEET))
+        def _():
+            @pl.loop(0, per)
+            def _(k):
+                hand(0, i, k).wait_recv()
+
+        @pl.when(z <= MEET)
+        def _():
+            fin[...] = rb[f1, 0, i]
+
+        @pl.when(z > MEET)
+        def _():
+            fin[...] = (rb[f1, 0, i].astype(F32) + rb[f2, 0, i].astype(F32)).astype(BF)
+
+        b, h = lax.rem(i // heads + yl, 2), lax.rem(i, heads)
+        qf = qf_buf[i]
+        num = nd_buf[i, :, :HD] + dot(qf, fin[:2 * HD])
+        ends = fin[2 * HD:].astype(F32)
+        nrm = jnp.concatenate(
+            [jnp.broadcast_to(ends[0:1], (HD, HD)), jnp.broadcast_to(ends[NORM:NORM + 1], (HD, HD))], axis=1).astype(BF)
+        den = nd_buf[i, :, HD:] + dot(qf, nrm, ((1,), (1,)))
+        out[b, :, pl.ds(pl.multiple_of(h * HD, HD), HD)] = (num / jnp.maximum(den, 1.0)).astype(BF)
 
     for cp in sent:
         cp.wait_send()
 
-    @pl.when(core == 0)
-    def _():
-        give.wait_send()
-
-    @pl.when(core == 1)
-    def _():
-        @pl.loop(0, pairs)
-        def _(i):
-            @pl.loop(0, per)
-            def _(k):
-                @pl.when(z < nseq - 1)
-                def _():
-                    hop(0, i, k).wait_send()
-                    hop(1, i, k).wait_send()
-
-                @pl.when(z > 0)
-                def _():
-                    hand(i, k).wait_send()
+    for t in range(2):
+        @pl.when((core == 0) | (z < SPLIT))
+        def _():
+            give(t).wait_send()
+
+    @pl.loop(0, pairs)
+    def _(i):
+        @pl.loop(0, per)
+        def _(k):
+            for s in range(2):
+                @pl.when((core == 1) & (z < nseq - 1))
+                def _():
+                    hop(flow, s, i, k, up, ob).wait_send()
+
+                @pl.when((core == 1) & (z >= SPLIT) & (z < MEET))
+                def _():
+                    hop(0, s, i, k, up, ob).wait_send()
+
+                @pl.when((core == 0) & ((z < SPLIT) | (z > MEET + 1)))
+                def _():
+                    hop(0, s, i, k, down, ob).wait_send()
+
+            @pl.when(((core == 1) & (z > 0)) | ((core == 0) & (z > MEET)))
+            def _():
+                hand(0, i, k).wait_send()
 
 
 def body(nseq, hidden_in, projection):
@@ -376,12 +461,12 @@
             vm((2, length, HD), F32), vm((2, length, nkv), BF),
             vm(wide, BF), vm(wide, BF), vm(wide, BF), vm(wide, F32),
             vm((pairs, block, HD), F32), vm((pairs, block, HD), F32),
-            vm((pairs, block, HD), BF), vm((pairs, block, HD), BF), vm((2, pairs, block, HD), BF),
+            vm((3, 2, pairs, block, HD), BF), vm((2, 2, pairs, block, HD), BF), vm((block, HD), BF),
             dma((1 + 2 * heads,)), dma((4,)), dma((4,)), dma((8,)), dma((8,)),
             dma((nseq // 2, 2, PIECES[0])), dma((nseq // 2, 2, PIECES[0])),
             dma((nseq // 2, 2, PIECES[1])), dma((nseq // 2, 2, PIECES[1])),
             dma((2, 2, 2)), dma((2, 2, 2)), dma((2, 2)), dma((2, 2)),
-            dma((2, pairs, per)), dma((2, pairs, per)), dma((1,)), dma((1,)), dma((pairs, per)), dma((pairs, per)),
+            dma((2, 2, pairs, per)), dma((2, 2, pairs, per)), dma((2,)), dma((2,)), dma((pairs, per)), dma((pairs, per)),
         ],
         compiler_params=pltpu.CompilerParams(
             collective_id=0, has_side_effects=True, vmem_limit_bytes=58 * 1024 * 1024),

time: 105 us -> 102 us (0.971); the launches traced: 105 us -> 101 us
  Pallas kernels: 103 us -> 98.9 us
    pallas_call x1, Pallas kernels: 103 us -> 98.9 us  [body(): pl.pallas_call(functools.partial(kernel, nseq), out_shape=jax.ShapeDtypeS...]
where the time goes in v3:
time: 102 us; the launch traced here: 101 us
  Pallas kernels  98.9 us (97%)
  local copies, waits for them, and re-layouts  1.71 us (2%)
    pallas_call x1, Pallas kernels, body(): pl.pallas_call(functools.partial(kernel, nseq), out_shape=jax.ShapeDtypeS...  98.9 us

profile of v3, /device:TPU:480, one launch (start us, length us, event | category | flops | bytes accessed | tf_op | source)
XLA Modules:
  0.0 100.6 jit_solution(15139074713688741804)
XLA Ops:
  0.0 98.9 %shard_map.28 = bf16[2,192,384]{2,1,0:T(8,128)(2,1)} custom-call(bf16[1,192,1536]{2,1,0:T(8,128)(2,1)} %hid.1, bf16[96,1152]{1,0:T(8,128)(2,1)} %proj.1), custom_call_target="tpu_custom_call" | custom-call | tf_op jit(solution)/shard_map/pallas_call | solution.py:451
  98.9 1.7 %copy.4 = bf16[2,192,384]{2,1,0:T(8,128)(2,1)} copy(bf16[2,192,384]{2,1,0:T(8,128)(2,1)} %shard_map.28) | data formatting | bytes 589824
